TPU v7x, 512 devices: a whole 4x4x16 slice. The times are simulated.
512 devices in a mesh: space: 32 (over z_lo, x), tm: 16 (over y, z_hi, core).
Axes of the slice: x: 4, y: 4, z: 16 (z_hi: 2, z_lo: 8; z = z_hi * 8 + z_lo), core: 2. Of those that a mesh axis runs over, the one named last changes fastest.
Arguments:
- adjoint_end: float32 [16, 11, 128, 2048], P('tm', None, 'space'), may hold values from -6 to 6
- depth_fwd: float32 [16, 4, 128, 2048], P('tm', None, 'space'), may hold values from 0.3 to 2
- velocity_fwd: float32 [16, 4, 2, 128, 2048], P('tm', None, None, 'space'), may hold values from -3 to 3
- salt_fwd: bfloat16 [16, 4, 8, 128, 2048], P('tm', None, None, 'space'), may hold values from -6 to 6
- wet_mask: int32 [16, 128, 2048], P('tm', 'space'), may hold values 0 or 1
- cell_class: int32 [128, 2048], P('space'), may hold values 0 or 1
- manning: float32 [128, 2048], P('space'), may hold values from 0.02 to 0.1
- conductivity: float32 [8, 128, 2048], P(None, 'space'), may hold values from 0.01 to 1
Outputs:
- adjoint_start: float32 [16, 11, 128, 2048], P('tm', None, 'space')
- manning_grad: float32 [128, 2048], P('space', 'tm')
- cond_grad: float32 [8, 128, 2048], P(None, 'space', 'tm')
Inputs may be any that keep to these rules, and one draw needn't show every extreme that they name: `wet_mask`: 1 marks a wet cell. `cell_class`: 1 marks a marsh cell, 0 a channel cell.
All inputs are finite; a program needn't handle non-finite values. No bound on the sum of `wet_mask` or of `cell_class` on one device may be relied on, other than what follows from the above.
Results may differ from a plain program's by a relative error of at most 0.0003.
Values sent between devices are 32-bit elements; how exact they have to be, the bound alone decides.
A program may use at most 64 MiB of HBM per device.

v0:
```python
import jax
import jax.numpy as jnp
from jax import lax
from jax.sharding import PartitionSpec as P

TIME_STEP = 0.4
GRAVITY = 9.81


def from_behind(value, axis, by):
    length = lax.axis_size(axis)
    pairs = [(i, i + by) for i in range(length) if 0 <= i + by < length]
    return lax.ppermute(value, axis, pairs)


def entering(value, axis, combine, identity):
    length, place = (lax.axis_size(axis), lax.axis_index(axis))
    everything = jax.tree.map(lambda part: lax.all_gather(part, axis), value)
    start = jax.tree.map(
        lambda part, zero: jnp.broadcast_to(jnp.asarray(zero, part.dtype), part.shape),
        value,
        identity,
    )

    def turn(k, before):
        at = length - 1 - k
        reached = at > place
        new = combine(before, jax.tree.map(lambda part: part[at], everything))
        return jax.tree.map(lambda a, b: jnp.where(reached, a, b), new, before)

    return lax.fori_loop(0, length, turn, start)


def split_up(value, dim, length):
    before, after = (value.shape[:dim], value.shape[dim + 1 :])
    return jnp.moveaxis(value.reshape(*before, length, -1, *after), dim, 0)


def sent_and_summed(value, axis, dim):
    blocks = split_up(value, dim, lax.axis_size(axis))
    arrived = lax.all_to_all(blocks, axis, split_axis=0, concat_axis=0, tiled=True)
    return arrived.sum(axis=0)


def lower_cols(quantity):
    zero_col = jnp.zeros_like(quantity[:, :1])
    return quantity - jnp.concatenate([zero_col, quantity[:, :-1]], 1)


def upper_cols(quantity):
    zero_col = jnp.zeros_like(quantity[:, :1])
    return jnp.concatenate([quantity[:, 1:], zero_col], 1) - quantity


def lower_rows(quantity):
    previous = from_behind(quantity[-1:], "space", 1)
    return quantity - jnp.concatenate([previous, quantity[:-1]], 0)


def upper_rows(quantity):
    following = from_behind(quantity[:1], "space", -1)
    return jnp.concatenate([quantity[1:], following], 0) - quantity


def friction(depth_now, velocity_now, manning):
    speed_now = jnp.sqrt(velocity_now[0] * velocity_now[0] + velocity_now[1] * velocity_now[1])
    powered = jnp.exp(4.0 / 3.0 * jnp.log(depth_now))
    friction_rate = GRAVITY * manning * manning * speed_now / powered
    return (speed_now, powered, friction_rate)


def salt_step(salt_adj, conductivity):
    zero_layer = jnp.zeros_like(salt_adj[:1])
    below_adj = jnp.concatenate([salt_adj[1:], zero_layer], 0)
    flux_down = conductivity * (below_adj - salt_adj)
    flux_up = jnp.concatenate([zero_layer, flux_down[:-1]], 0)
    return salt_adj + TIME_STEP * (flux_down - flux_up)


def body(
    adjoint_end, depth_fwd, velocity_fwd, salt_fwd, wet_mask, cell_class, manning, conductivity
):
    own_end = adjoint_end[0]
    depth_win = depth_fwd[0]
    velocity_win = velocity_fwd[0]
    salt_win = salt_fwd[0]
    wet_f = wet_mask[0].astype(jnp.float32)
    infiltration = wet_f * (0.25 + 0.75 * cell_class.astype(jnp.float32))
    surface_adj = own_end[0]
    flow_x = own_end[1]
    flow_y = own_end[2]
    salt_adj = own_end[3:]
    grad_n = jnp.zeros_like(surface_adj)
    grad_k = jnp.zeros_like(salt_adj)
    steps_total = depth_win.shape[0]
    first_rate = None
    for step_now in range(steps_total - 1, -1, -1):
        depth_now = depth_win[step_now]
        velocity_now = velocity_win[step_now]
        speed_now, powered, friction_rate = friction(depth_now, velocity_now, manning)
        if step_now == 0:
            first_rate = friction_rate
        relaxed = 1.0 + TIME_STEP * friction_rate
        damping = wet_f / relaxed
        grad_n = grad_n - 2.0 * TIME_STEP * GRAVITY * manning * speed_now * (
            velocity_now[0] * flow_x + velocity_now[1] * flow_y
        ) * damping / (powered * relaxed)
        salt_now = salt_win[step_now].astype(jnp.float32)
        zero_layer = jnp.zeros_like(salt_now[:1])
        salt_below = jnp.concatenate([salt_now[1:], zero_layer], 0)
        adj_below = jnp.concatenate([salt_adj[1:], zero_layer], 0)
        grad_k = grad_k + TIME_STEP * (salt_below - salt_now) * (salt_adj - adj_below)
        level_mid = (
            surface_adj
            + TIME_STEP * lower_rows(depth_now * damping * flow_x)
            + TIME_STEP * lower_cols(depth_now * damping * flow_y)
        )
        wet_mid = wet_f * level_mid
        flow_x = damping * flow_x + TIME_STEP * upper_rows(wet_mid)
        flow_y = damping * flow_y + TIME_STEP * upper_cols(wet_mid)
        surface_adj = level_mid + TIME_STEP * infiltration * salt_adj[0]
        salt_adj = salt_step(salt_adj, conductivity)
    flow_factor = wet_f / (1.0 + steps_total * TIME_STEP * first_rate)
    cond_above = jnp.concatenate([jnp.zeros_like(conductivity[:1]), conductivity[:-1]], 0)
    salt_factor = 1.0 / (1.0 + steps_total * TIME_STEP * (conductivity + cond_above))
    coarse = jnp.concatenate(
        [jnp.ones_like(surface_adj)[None], flow_factor[None], flow_factor[None], salt_factor], 0
    )
    fine_start = jnp.concatenate([surface_adj[None], flow_x[None], flow_y[None], salt_adj], 0)
    offset = fine_start - coarse * own_end
    is_last = lax.axis_index("tm") == lax.axis_size("tm") - 1
    factor_own = jnp.where(is_last, jnp.zeros_like(coarse), coarse)
    offset_own = jnp.where(is_last, coarse * own_end + offset, offset)

    def compose_maps(earlier, later):
        return (later[0] * earlier[0], later[0] * earlier[1] + later[1])

    identity_pair = (jnp.ones_like(coarse), jnp.zeros_like(coarse))
    acc_factor, acc_offset = entering((factor_own, offset_own), "tm", compose_maps, identity_pair)
    end_new = acc_factor * own_end + acc_offset
    start_new = coarse * end_new + offset
    stacked = jnp.concatenate([grad_n[None], grad_k], 0)
    own_share = sent_and_summed(stacked, "tm", 2)
    return (start_new[None], own_share[0], own_share[1:])


def solution(mesh):
    return jax.shard_map(
        body,
        mesh=mesh,
        in_specs=(
            P("tm", None, "space", None),
            P("tm", None, "space", None),
            P("tm", None, None, "space", None),
            P("tm", None, None, "space", None),
            P("tm", "space", None),
            P("space", None),
            P("space", None),
            P(None, "space", None),
        ),
        out_specs=(P("tm", None, "space", None), P("space", "tm"), P(None, "space", "tm")),
        check_vma=False,
    )
```

profile of v0, /device:TPU:1, one launch (start us, length us, event | category | flops | bytes accessed | tf_op | source)
XLA Modules:
  0.0 396.4 jit_solution(5669040742824051408)
XLA Ops:
  7.3 1.0 bitcast_multiply_fusion.16
  8.3 0.8 bitcast_multiply_fusion.19
  9.1 3.9 collective-permute-start
  13.0 1.0 slice_bitcast_fusion.4
  14.0 1.1 fusion.17
  15.1 1.1 bitcast_add_fusion.1
  16.2 1.2 slice_convert_fusion.3
  17.6 0.1 subtract_multiply_fusion.2
  17.7 0.1 bitcast_multiply_fusion.31
  17.8 0.1 slice.341
  17.9 1.3 collective-permute-start.1
  19.2 0.1 fusion.81
  19.4 2.9 collective-permute-done.1
  22.4 3.1 collective-permute-start.2
  25.5 0.1 multiply_add_fusion.2
  25.6 0.6 collective-permute-done.2
  26.3 0.1 bitcast_multiply_fusion.30
  26.4 0.1 slice.349
  26.5 1.3 collective-permute-start.3
  27.8 0.1 fusion.83
  27.9 3.2 collective-permute-done.3
  31.2 4.8 %collective-permute-start.4 = (f32[1,2048]{1,0:T(1,128)S(1)}, f32[1,2048]{1,0:T(1,128)S(1)}, u32[]{:S(2)}, u32[]{:S(2)}) collective-permute-start(f32[1,2048]{1,0:T(1,128)S(1)} %slice.347), channel_id=1, source_target_pairs={{0,16},{16,32},{32,48},{48,64},{64,80},{80,96},{96,112},{112,128},... | collective-permute-start | bytes 24584 | tf_op jit(solution)/shard_map/ppermute | solution.py:13
  36.0 0.1 subtract_multiply_fusion.1
  36.1 0.6 collective-permute-done.4
  36.7 0.1 bitcast_multiply_fusion.29
  36.8 1.3 collective-permute-start.5
  38.1 0.1 multiply_add_fusion.1
  38.3 0.1 slice.358
  38.4 3.1 collective-permute-done.5
  41.5 0.3 subtract_bitcast_fusion
  41.8 5.5 %collective-permute-start.6 = (f32[1,2048]{1,0:T(1,128)S(1)}, f32[1,2048]{1,0:T(1,128)S(1)}, u32[]{:S(2)}, u32[]{:S(2)}) collective-permute-start(f32[1,2048]{1,0:T(1,128)S(1)} %slice.356), channel_id=1, source_target_pairs={{0,16},{16,32},{32,48},{48,64},{64,80},{80,96},{96,112},{112,128},... | collective-permute-start | bytes 24584 | tf_op jit(solution)/shard_map/ppermute | solution.py:13
  47.3 0.8 fusion.8
  48.2 0.1 fusion.86
  48.4 1.3 collective-permute-start.7
  49.7 0.1 multiply_add_fusion
  49.8 0.1 slice.365
  49.9 3.1 collective-permute-done.7
  53.1 1.1 add_select_fusion
  54.3 0.7 all-gather.3.cloned.1.call-update
  55.0 0.8 maximum_bitcast_fusion
  55.8 24.9 %all-to-all-start = ((f32[16,9,4,128]{3,2,1,0:T(4,128)}), f32[16,9,4,128]{3,2,1,0:T(4,128)S(1)}, u32[]{:S(2)}, u32[]{:S(2)}) async-start(f32[16,9,4,128]{3,2,1,0:T(4,128)} %maximum_bitcast_fusion), calls=%async_computation | async-start | bytes 589824 | tf_op jit(solution)/shard_map/all_to_all | solution.py:41
  80.7 16.3 %all-to-all-done = f32[16,9,4,128]{3,2,1,0:T(4,128)S(1)} async-done(((f32[16,9,4,128]{3,2,1,0:T(4,128)}), f32[16,9,4,128]{3,2,1,0:T(4,128)S(1)}, u32[]{:S(2)}, u32[]{:S(2)}) %all-to-all-start) | async-done | bytes 294944 | tf_op jit(solution)/shard_map/all_to_all | solution.py:41
  97.0 0.6 slice.373
  97.6 0.6 slice_bitcast_fusion.8
  98.2 127.8 %all-gather.5.cloned.1.call-done = f32[16,11,4,2048]{3,2,1,0:T(4,128)} async-done(((f32[1,11,4,2048]{3,2,1,0:T(4,128)}), f32[16,11,4,2048]{3,2,1,0:T(4,128)}) %all-gather.5.cloned.1.call-update) | async-done | bytes 5767184 | tf_op jit(solution)/shard_map/all_gather | solution.py:18
  226.0 137.1 %all-gather.3.cloned.1.call-done = f32[16,11,4,2048]{3,2,1,0:T(4,128)} async-done(((f32[1,11,4,2048]{3,2,1,0:T(4,128)}), f32[16,11,4,2048]{3,2,1,0:T(4,128)}) %all-gather.3.cloned.1.call-update) | async-done | bytes 5767184 | tf_op jit(solution)/shard_map/all_gather | solution.py:18
  363.0 25.4 %while.18 = (s32[]{:T(128)}, f32[11,4,2048]{2,1,0:T(4,128)S(1)}, f32[11,4,2048]{2,1,0:T(4,128)S(1)}, s32[]{:T(128)}, f32[16,11,4,2048]{3,2,1,0:T(4,128)}, /*inde...) while((s32[]{:T(128)}, f32[11,4,2048]{2,1,0:T(4,128)S(1)}, ...), condition=%wide.region_1.2_spmd.clone, body=%wide.region_0.1_spmd.clone.sunk | while | flops 630792 | bytes 2162867 | solution.py:31
  363.0 1.6 fusion.97
  364.6 1.6 fusion.97
  366.2 1.6 fusion.97
  367.8 1.6 fusion.97
  369.4 1.6 fusion.97
  371.0 1.6 fusion.97
  372.6 1.6 fusion.97
  374.2 1.6 fusion.97
  375.8 1.6 fusion.97
  377.3 1.6 fusion.97
  378.9 1.6 fusion.97
  380.5 1.6 fusion.97
  382.1 1.6 fusion.97
  383.7 1.6 fusion.97
  385.3 1.6 fusion.97
  386.9 1.6 fusion.97
  388.4 1.1 fusion.2
  (54 shorter events, 0.8 us)
Async XLA Ops:
  7.2 10.5 %copy-start = (f32[1,11,4,2048]{3,2,1,0:T(4,128)S(1)}, f32[1,11,4,2048]{3,2,1,0:T(4,128)}, u32[]{:S(2)}) copy-start(f32[1,11,4,2048]{3,2,1,0:T(4,128)} %param.10) | copy-start | bytes 1081348
  7.2 10.5 %copy-start.3 = (s32[1,4,2048]{2,1,0:T(4,128)S(1)}, s32[1,4,2048]{2,1,0:T(4,128)}, u32[]{:S(2)}) copy-start(s32[1,4,2048]{2,1,0:T(4,128)} %param.14) | copy-start | bytes 98308
  7.2 12.0 %copy-start.4 = (f32[1,4,4,2048]{3,2,1,0:T(4,128)S(1)}, f32[1,4,4,2048]{3,2,1,0:T(4,128)}, u32[]{:S(2)}) copy-start(f32[1,4,4,2048]{3,2,1,0:T(4,128)} %param.11) | copy-start | bytes 393220
  7.2 12.0 %copy-start.6 = (f32[4,2048]{1,0:T(4,128)S(1)}, f32[4,2048]{1,0:T(4,128)}, u32[]{:S(2)}) copy-start(f32[4,2048]{1,0:T(4,128)} %param.16) | copy-start | bytes 98308
  7.2 12.0 %copy-start.5 = (f32[1,4,2,4,2048]{4,3,2,1,0:T(4,128)S(1)}, f32[1,4,2,4,2048]{4,3,2,1,0:T(4,128)}, u32[]{:S(2)}) copy-start(f32[1,4,2,4,2048]{4,3,2,1,0:T(4,128)} %param.12) | copy-start | bytes 786436
  7.2 10.3 %copy-start.1 = (f32[8,4,2048]{2,1,0:T(4,128)S(1)}, f32[8,4,2048]{2,1,0:T(4,128)}, u32[]{:S(2)}) copy-start(f32[8,4,2048]{2,1,0:T(4,128)} %param.17) | copy-start | bytes 786436
  7.2 19.0 %copy-start.7 = (s32[4,2048]{1,0:T(4,128)S(1)}, s32[4,2048]{1,0:T(4,128)}, u32[]{:S(2)}) copy-start(s32[4,2048]{1,0:T(4,128)} %param.15) | copy-start | bytes 98308
  7.2 218.8 %all-gather.5.cloned.1.call-start = ((), (), s32[]{:S(2)}) async-start(), calls=%async_computation.2 | async-start | bytes 6127616 | tf_op jit(solution)/shard_map/all_gather | solution.py:18
  9.1 8.6 %collective-permute-start = (f32[1,2048]{1,0:T(1,128)S(1)}, f32[1,2048]{1,0:T(1,128)S(1)}, u32[]{:S(2)}, u32[]{:S(2)}) collective-permute-start(f32[1,2048]{1,0:T(1,128)S(1)} %slice.334), channel_id=1, source_target_pairs={{0,16},{16,32},{32,48},{48,64},{64,80},{80,96},{96,112},{112,128},... | collective-permute-start | bytes 24584 | tf_op jit(solution)/shard_map/ppermute | solution.py:13
  17.5 29.8 %slice-start = ((f32[8,4,2048]{2,1,0:T(4,128)}), f32[7,4,2048]{2,1,0:T(4,128)S(1)}, s32[]{:S(2)}) async-start(f32[8,4,2048]{2,1,0:T(4,128)} %param.17), calls=%async_computation.3 | async-start | bytes 458752 | tf_op jit(solution)/shard_map/slice | solution.py:124
  17.5 29.8 %copy-start.2 = (bf16[1,4,8,4,2048]{4,3,2,1,0:T(4,128)(2,1)S(1)}, bf16[1,4,8,4,2048]{4,3,2,1,0:T(4,128)(2,1)}, u32[]{:S(2)}) copy-start(bf16[1,4,8,4,2048]{4,3,2,1,0:T(4,128)(2,1)} %param.13) | copy-start | bytes 1572868
  17.9 4.4 %collective-permute-start.1 = (f32[1,2048]{1,0:T(1,128)S(1)}, f32[1,2048]{1,0:T(1,128)S(1)}, u32[]{:S(2)}, u32[]{:S(2)}) collective-permute-start(f32[1,2048]{1,0:T(1,128)S(1)} %slice.338), channel_id=1, source_target_pairs={{16,0},{32,16},{48,32},{64,48},{80,64},{96,80},{112,96},{128,112},... | collective-permute-start | bytes 24584 | tf_op jit(solution)/shard_map/ppermute | solution.py:13
  22.4 3.9 collective-permute-start.2
  26.5 4.6 %collective-permute-start.3 = (f32[1,2048]{1,0:T(1,128)S(1)}, f32[1,2048]{1,0:T(1,128)S(1)}, u32[]{:S(2)}, u32[]{:S(2)}) collective-permute-start(f32[1,2048]{1,0:T(1,128)S(1)} %slice.346), channel_id=1, source_target_pairs={{16,0},{32,16},{48,32},{64,48},{80,64},{96,80},{112,96},{128,112},... | collective-permute-start | bytes 24584 | tf_op jit(solution)/shard_map/ppermute | solution.py:13
  31.2 5.6 %collective-permute-start.4 = (f32[1,2048]{1,0:T(1,128)S(1)}, f32[1,2048]{1,0:T(1,128)S(1)}, u32[]{:S(2)}, u32[]{:S(2)}) collective-permute-start(f32[1,2048]{1,0:T(1,128)S(1)} %slice.347), channel_id=1, source_target_pairs={{0,16},{16,32},{32,48},{48,64},{64,80},{80,96},{96,112},{112,128},... | collective-permute-start | bytes 24584 | tf_op jit(solution)/shard_map/ppermute | solution.py:13
  36.8 4.7 %collective-permute-start.5 = (f32[1,2048]{1,0:T(1,128)S(1)}, f32[1,2048]{1,0:T(1,128)S(1)}, u32[]{:S(2)}, u32[]{:S(2)}) collective-permute-start(f32[1,2048]{1,0:T(1,128)S(1)} %slice.355), channel_id=1, source_target_pairs={{16,0},{32,16},{48,32},{64,48},{80,64},{96,80},{112,96},{128,112},... | collective-permute-start | bytes 24584 | tf_op jit(solution)/shard_map/ppermute | solution.py:13
  41.8 6.4 %collective-permute-start.6 = (f32[1,2048]{1,0:T(1,128)S(1)}, f32[1,2048]{1,0:T(1,128)S(1)}, u32[]{:S(2)}, u32[]{:S(2)}) collective-permute-start(f32[1,2048]{1,0:T(1,128)S(1)} %slice.356), channel_id=1, source_target_pairs={{0,16},{16,32},{32,48},{48,64},{64,80},{80,96},{96,112},{112,128},... | collective-permute-start | bytes 24584 | tf_op jit(solution)/shard_map/ppermute | solution.py:13
  48.4 4.7 %collective-permute-start.7 = (f32[1,2048]{1,0:T(1,128)S(1)}, f32[1,2048]{1,0:T(1,128)S(1)}, u32[]{:S(2)}, u32[]{:S(2)}) collective-permute-start(f32[1,2048]{1,0:T(1,128)S(1)} %slice.364), channel_id=1, source_target_pairs={{16,0},{32,16},{48,32},{64,48},{80,64},{96,80},{112,96},{128,112},... | collective-permute-start | bytes 24584 | tf_op jit(solution)/shard_map/ppermute | solution.py:13
  54.2 308.8 %all-gather.3.cloned.1.call-start = ((), (), s32[]{:S(2)}) async-start(), calls=%async_computation.1 | async-start | bytes 6127616 | tf_op jit(solution)/shard_map/all_gather | solution.py:18
  55.8 41.1 %all-to-all-start = ((f32[16,9,4,128]{3,2,1,0:T(4,128)}), f32[16,9,4,128]{3,2,1,0:T(4,128)S(1)}, u32[]{:S(2)}, u32[]{:S(2)}) async-start(f32[16,9,4,128]{3,2,1,0:T(4,128)} %maximum_bitcast_fusion), calls=%async_computation | async-start | bytes 589824 | tf_op jit(solution)/shard_map/all_to_all | solution.py:41
Sparse Core Ops, SparseCore 0:
  54.3 171.6 all-gather.4
  229.3 133.7 all-gather.2
where the time goes:
time: 397 us; the launch traced here: 396 us
  waiting for transfers between devices  295 us (74%)
  starting transfers between devices  47.4 us (12%)
  other arithmetic  35.6 us (9%)
  between operations  14.6 us (4%)
    all_gather x2, waiting for transfers between devices, entering(): everything = jax.tree.map(lambda part: lax.all_gather(part, axis), value)  265 us
    select_n x16, other arithmetic, turn(): return jax.tree.map(lambda a, b: jnp.where(reached, a, b), new, before)  24.9 us
    all_to_all x1, starting transfers between devices, sent_and_summed(): lax.all_to_all(blocks, axis, split_axis=0, concat_axis=0, tiled=True)  24.9 us
    ppermute x8, starting transfers between devices, from_behind(): return lax.ppermute(value, axis, pairs)  22.5 us
    all_to_all x1, waiting for transfers between devices, sent_and_summed(): lax.all_to_all(blocks, axis, split_axis=0, concat_axis=0, tiled=True)  16.3 us
    ppermute x8, waiting for transfers between devices, from_behind(): return lax.ppermute(value, axis, pairs)  13.7 us
  transfers between devices with their start and end apart: 11, of which 9 were waited for; matrix products, arithmetic and copies ran while one was open for 2% of the time, Pallas kernels for 0%

commit v1 on v0

v1 whole, which is shorter than its diff:
```python
import jax
import jax.numpy as jnp
from jax import lax
from jax.experimental import pallas as pl
from jax.experimental.pallas import tpu as pltpu
from jax.sharding import PartitionSpec as P

TIME_STEP = 0.4
GRAVITY = 9.81
MESH = pl.DeviceIdType.MESH
F32 = jnp.float32


def remote(src, dst, send_sem, recv_sem, device):
    return pltpu.make_async_remote_copy(
        src_ref=src, dst_ref=dst, send_sem=send_sem, recv_sem=recv_sem,
        device_id=device, device_id_type=MESH,
    )


def kernel(
    space_n, end_ref, depth_ref, vel_ref, salt_ref, wet_ref, cls_ref, man_ref, cond_ref,
    out_ref, gn_ref, gk_ref,
    damp, hdamp, gcoef, source, off_s, fac_s, off_f, grads,
    down_out, up_out, down_in, up_in,
    core_s, core_f, pair_s, pair_f, z_s, z_f, quad_s, quad_f, y_s, y_f,
    zb_s_out, zb_f_out, zb_s, zb_f, eh_s, eh_f, cb_s_out, cb_f_out, cb_s, cb_f,
    core_g, sum_g, y_g, z_g_out, z_g,
    halo_sems, core_sems, z_sems, y_sems, yg_sems, zb_sems, cb_sems,
):
    sp = lax.axis_index("space")
    w = lax.axis_index("tm")
    core = lax.rem(w, 2)
    zh = lax.rem(lax.div(w, 2), 2)
    y = lax.div(w, 4)
    core_peer = (sp, w + 1 - 2 * core)
    z_peer = (sp, w + 2 - 4 * zh)
    has_prev = sp > 0
    has_next = sp < space_n - 1

    def y_peer(d):
        return (sp, lax.rem(w + 4 * d, 16))

    barrier = pltpu.get_barrier_semaphore()
    for peer in (core_peer, z_peer, y_peer(1), y_peer(2), y_peer(3)):
        pl.semaphore_signal(barrier, inc=1, device_id=peer, device_id_type=MESH)

    @pl.when(has_prev)
    def _():
        pl.semaphore_signal(barrier, inc=1, device_id=(sp - 1, w), device_id_type=MESH)

    @pl.when(has_next)
    def _():
        pl.semaphore_signal(barrier, inc=1, device_id=(sp + 1, w), device_id_type=MESH)

    last = jnp.where(w == 15, 1.0, 0.0).astype(F32)

    def chunk(i, carry):
        block = lax.div(i, 4)
        g_core = lax.rem(i, 2)
        g_zh = lax.rem(lax.div(i, 2), 2)
        cols = pl.ds(pl.multiple_of(i * 128, 128), 128)
        sub = pl.ds(pl.multiple_of(lax.rem(i, 4) * 128, 128), 128)
        wet = wet_ref[0, :, cols].astype(F32)
        infil = TIME_STEP * wet * (0.25 + 0.75 * cls_ref[:, cols].astype(F32))
        man = man_ref[:, cols]
        cond = cond_ref[:, :, cols]
        mu = end_ref[0, 3:, :, cols]
        zero = jnp.zeros_like(mu[:1])
        cond_above = jnp.concatenate([zero, cond[:-1]], 0)
        factor = 1.0 / (1.0 + 4 * TIME_STEP * (cond + cond_above))
        gk = jnp.zeros_like(mu)
        start = mu
        for k in (3, 2, 1, 0):
            h = depth_ref[0, k, :, cols]
            u = vel_ref[0, k, 0, :, cols]
            v = vel_ref[0, k, 1, :, cols]
            speed = jnp.sqrt(u * u + v * v)
            powered = jnp.exp(4.0 / 3.0 * jnp.log(h))
            rate = GRAVITY * man * man * speed / powered
            relaxed = 1.0 + TIME_STEP * rate
            damping = wet / relaxed
            damp[k, :, cols] = damping
            hdamp[k, :, cols] = h * damping
            gcoef[k, :, cols] = (
                -2.0 * TIME_STEP * GRAVITY * man * speed * damping / (powered * relaxed)
            )
            if k == 0:
                off_f[block, 3, :, sub] = wet / (1.0 + 4 * TIME_STEP * rate)
            source[k, :, cols] = infil * mu[0]
            salt = salt_ref[0, k, :, :, cols].astype(F32)
            salt_below = jnp.concatenate([salt[1:], zero], 0)
            mu_below = jnp.concatenate([mu[1:], zero], 0)
            diff = mu_below - mu
            gk = gk - TIME_STEP * (salt_below - salt) * diff
            flux = cond * diff
            mu = mu + TIME_STEP * (flux - jnp.concatenate([zero, flux[:-1]], 0))
        held = factor * start
        offset = mu - held
        off_s[block, :, :, sub] = offset + last * held
        fac_s[block, :, :, sub] = factor
        grads[g_core, block, g_zh, 0:8] = gk
        return carry

    lax.fori_loop(0, 16, chunk, 0)

    for d in (1, 2, 3):
        @pl.when(y + d > 3)
        def _(d=d):
            y_s[d - 1] = jnp.zeros(y_s.shape[1:], F32)
            y_f[d - 1] = jnp.zeros(y_f.shape[1:], F32)

    @pl.when(sp == 0)
    def _():
        down_in[...] = jnp.zeros(down_in.shape, F32)

    @pl.when(sp == space_n - 1)
    def _():
        up_in[...] = jnp.zeros(up_in.shape, F32)

    pl.semaphore_wait(
        barrier, 5 + jnp.where(has_prev, 1, 0) + jnp.where(has_next, 1, 0)
    )

    other_half = pl.ds(2 * (1 - core), 2)
    copy_core_s = remote(
        off_s.at[other_half], core_s, core_sems.at[0, 0], core_sems.at[1, 0], core_peer
    )
    copy_core_s.start()
    copy_z_s = remote(pair_s.at[1 - zh], z_s, z_sems.at[0, 0], z_sems.at[1, 0], z_peer)
    copy_z_f = remote(pair_f.at[1 - zh], z_f, z_sems.at[0, 1], z_sems.at[1, 1], z_peer)

    def pair_salt():
        copy_core_s.wait_recv()
        for b in range(2):
            mine = off_s[2 * core + b]
            theirs = core_s[b]
            earlier = jnp.where(core == 0, mine, theirs)
            later = jnp.where(core == 0, theirs, mine)
            pair_s[b] = earlier + fac_s[2 * core + b] * later
        copy_z_s.start()

    level = end_ref[0, 0]
    flow_x = end_ref[0, 1]
    flow_y = end_ref[0, 2]
    wet = wet_ref[0].astype(F32)
    lanes = lax.broadcasted_iota(jnp.int32, level.shape, 1)
    n_cols = level.shape[1]
    grad_n = jnp.zeros_like(level)
    halo_copies = []
    for turn, k in enumerate((3, 2, 1, 0)):
        hdx = hdamp[k] * flow_x
        hdy = hdamp[k] * flow_y
        hdy_left = jnp.where(lanes == 0, 0.0, pltpu.roll(hdy, 1, 1))
        partial = level + TIME_STEP * hdx + TIME_STEP * (hdy - hdy_left)
        down_out[turn] = hdx[3:4]
        up_out[turn, 0:1] = wet[0:1] * partial[0:1]
        up_out[turn, 1:2] = wet[0:1]
        down = remote(
            down_out.at[turn], down_in.at[turn],
            halo_sems.at[0, turn], halo_sems.at[1, turn], (sp + 1, w),
        )
        up = remote(
            up_out.at[turn], up_in.at[turn],
            halo_sems.at[2, turn], halo_sems.at[3, turn], (sp - 1, w),
        )
        halo_copies.append((down, up))

        @pl.when(has_next)
        def _(down=down):
            down.start()

        @pl.when(has_prev)
        def _(up=up):
            up.start()

        if turn == 0:
            pair_salt()
        grad_n = grad_n + gcoef[k] * (vel_ref[0, k, 0] * flow_x + vel_ref[0, k, 1] * flow_y)

        @pl.when(has_prev)
        def _(down=down):
            down.wait_recv()

        @pl.when(has_next)
        def _(up=up):
            up.wait_recv()

        before = jnp.concatenate([down_in[turn], hdx[0:3]], 0)
        mid = partial - TIME_STEP * before
        wet_mid = wet * mid
        after_row = up_in[turn, 0:1] - TIME_STEP * up_in[turn, 1:2] * hdx[3:4]
        after = jnp.concatenate([wet_mid[1:4], after_row], 0)
        right = jnp.where(lanes == n_cols - 1, 0.0, pltpu.roll(wet_mid, n_cols - 1, 1))
        damping = damp[k]
        flow_x = damping * flow_x + TIME_STEP * (after - wet_mid)
        flow_y = damping * flow_y + TIME_STEP * (right - wet_mid)
        level = mid + source[k]

    for b in range(4):
        cols = slice(b * 512, b * 512 + 512)
        factor = off_f[b, 3]
        off_f[b, 0] = level[:, cols] - (1.0 - last) * end_ref[0, 0, :, cols]
        off_f[b, 1] = flow_x[:, cols] - (1.0 - last) * factor * end_ref[0, 1, :, cols]
        off_f[b, 2] = flow_y[:, cols] - (1.0 - last) * factor * end_ref[0, 2, :, cols]
    copy_core_f = remote(
        off_f.at[other_half], core_f, core_sems.at[0, 1], core_sems.at[1, 1], core_peer
    )
    copy_core_f.start()
    for i in range(16):
        grads[i % 2, i // 4, i // 2 % 2, 8] = grad_n[:, i * 128 : i * 128 + 128]
    copy_core_g = remote(
        grads.at[1 - core], core_g, core_sems.at[0, 2], core_sems.at[1, 2], core_peer
    )
    copy_core_g.start()

    copy_core_f.wait_recv()
    for b in range(2):
        mine = off_f[2 * core + b]
        theirs = core_f[b]
        earlier = jnp.where(core == 0, mine, theirs)
        later = jnp.where(core == 0, theirs, mine)
        pair_f[b, 0] = earlier[0] + later[0]
        pair_f[b, 1] = earlier[1] + earlier[3] * later[1]
        pair_f[b, 2] = earlier[2] + earlier[3] * later[2]
        pair_f[b, 3] = earlier[3] * later[3]
    copy_z_f.start()

    def y_copies(quad, slots, which):
        return [
            remote(
                quad, slots.at[d - 1], y_sems.at[0, which, d - 1], y_sems.at[1, which, d - 1],
                y_peer(4 - d),
            )
            for d in (1, 2, 3)
        ]

    def start_down(copies):
        for d in (1, 2, 3):
            @pl.when(y >= d)
            def _(d=d):
                copies[d - 1].start()

    def wait_down(copies):
        for d in (1, 2, 3):
            @pl.when(y + d <= 3)
            def _(d=d):
                copies[d - 1].wait_recv()

    own = 2 * core + zh
    copy_z_s.wait_recv()
    factor = fac_s[own]
    pair_factor = factor * factor
    mine = pair_s[zh]
    theirs = z_s[...]
    pair_first = jnp.where(zh == 0, mine, theirs)
    pair_second = jnp.where(zh == 0, theirs, mine)
    quad_s[...] = pair_first + pair_factor * pair_second
    copies_y_s = y_copies(quad_s, y_s, 0)
    start_down(copies_y_s)

    copy_core_g.wait_recv()
    sum_g[...] = grads[core] + core_g[...]
    copies_y_g = []
    for d in (1, 2, 3):
        copy = remote(
            sum_g.at[lax.rem(y + d, 4)], y_g.at[d - 1],
            yg_sems.at[0, d - 1], yg_sems.at[1, d - 1], y_peer(d),
        )
        copy.start()
        copies_y_g.append(copy)

    copy_zb_s = remote(zb_s_out, zb_s, zb_sems.at[0, 0], zb_sems.at[1, 0], z_peer)
    copy_zb_f = remote(zb_f_out, zb_f, zb_sems.at[0, 1], zb_sems.at[1, 1], z_peer)
    copy_zb_g = remote(z_g_out.at[1 - zh], z_g, zb_sems.at[0, 2], zb_sems.at[1, 2], z_peer)

    wait_down(copies_y_s)
    factor = fac_s[own]
    pair_factor = factor * factor
    quad_factor = pair_factor * pair_factor
    at_second = y_s[0] + quad_factor * (y_s[1] + quad_factor * y_s[2])
    mine = pair_s[zh]
    theirs = z_s[...]
    at_first = jnp.where(zh == 0, theirs, mine) + pair_factor * at_second
    eh_s[zh] = jnp.where(zh == 0, at_first, at_second)
    zb_s_out[...] = jnp.where(zh == 0, at_second, at_first)
    copy_zb_s.start()

    copy_z_f.wait_recv()
    mine = pair_f[zh]
    theirs = z_f[...]
    first_f = jnp.where(zh == 0, mine, theirs)
    second_f = jnp.where(zh == 0, theirs, mine)
    quad_f[0] = first_f[0] + second_f[0]
    quad_f[1] = first_f[1] + first_f[3] * second_f[1]
    quad_f[2] = first_f[2] + first_f[3] * second_f[2]
    quad_f[3] = first_f[3] * second_f[3]
    copies_y_f = y_copies(quad_f, y_f, 1)
    start_down(copies_y_f)

    total = sum_g[y]
    for d in (1, 2, 3):
        copies_y_g[d - 1].wait_recv()
        total = total + y_g[d - 1]
    z_g_out[...] = total
    copy_zb_g.start()

    wait_down(copies_y_f)
    mine = pair_f[zh]
    theirs = z_f[...]
    second_f = jnp.where(zh == 0, theirs, mine)
    for field in range(3):
        if field == 0:
            at_second = y_f[0, 0] + y_f[1, 0] + y_f[2, 0]
            at_first = second_f[0] + at_second
        else:
            at_second = y_f[0, field] + y_f[0, 3] * (
                y_f[1, field] + y_f[1, 3] * y_f[2, field]
            )
            at_first = second_f[field] + second_f[3] * at_second
        eh_f[zh, field] = jnp.where(zh == 0, at_first, at_second)
        zb_f_out[field] = jnp.where(zh == 0, at_second, at_first)
    copy_zb_f.start()

    copy_zb_s.wait_recv()
    eh_s[1 - zh] = zb_s[...]
    for b in range(2):
        late = eh_s[b]
        mine = off_s[2 * core + b]
        theirs = core_s[b]
        early = jnp.where(core == 0, theirs, mine) + fac_s[2 * core + b] * late
        cb_s_out[b] = jnp.where(core == 0, late, early)
        eh_s[b] = jnp.where(core == 0, early, late)
    copy_cb_s = remote(cb_s_out, cb_s, cb_sems.at[0, 0], cb_sems.at[1, 0], core_peer)
    copy_cb_s.start()
    for b in range(2):
        block = 2 * core + b
        cols = pl.ds(pl.multiple_of(block * 512, 512), 512)
        out_ref[0, 3:, :, cols] = off_s[block] + fac_s[block] * eh_s[b]

    copy_zb_f.wait_recv()
    eh_f[1 - zh] = zb_f[...]
    for b in range(2):
        mine = off_f[2 * core + b]
        theirs = core_f[b]
        late_map = jnp.where(core == 0, theirs, mine)
        for field in range(3):
            late = eh_f[b, field]
            if field == 0:
                early = late_map[0] + late
            else:
                early = late_map[field] + late_map[3] * late
            cb_f_out[b, field] = jnp.where(core == 0, late, early)
            eh_f[b, field] = jnp.where(core == 0, early, late)
    copy_cb_f = remote(cb_f_out, cb_f, cb_sems.at[0, 1], cb_sems.at[1, 1], core_peer)
    copy_cb_f.start()

    copy_zb_g.wait_recv()
    total = z_g_out[zh] + z_g[...]
    gk_ref[...] = total[0:8]
    gn_ref[...] = total[8]

    copy_cb_s.wait_recv()
    for b in range(2):
        block = 2 * (1 - core) + b
        cols = pl.ds(pl.multiple_of(block * 512, 512), 512)
        out_ref[0, 3:, :, cols] = off_s[block] + fac_s[block] * cb_s[b]
    copy_cb_f.wait_recv()
    for half in range(2):
        for b in range(2):
            block = 2 * core + b if half == 0 else 2 * (1 - core) + b
            cols = pl.ds(pl.multiple_of(block * 512, 512), 512)
            ends = eh_f if half == 0 else cb_f
            factor = off_f[block, 3]
            out_ref[0, 0, :, cols] = off_f[block, 0] + ends[b, 0]
            out_ref[0, 1, :, cols] = off_f[block, 1] + factor * ends[b, 1]
            out_ref[0, 2, :, cols] = off_f[block, 2] + factor * ends[b, 2]

    for down, up in halo_copies:
        @pl.when(has_next)
        def _(down=down):
            down.wait_send()

        @pl.when(has_prev)
        def _(up=up):
            up.wait_send()

    for d in (1, 2, 3):
        @pl.when(y >= d)
        def _(d=d):
            copies_y_s[d - 1].wait_send()
            copies_y_f[d - 1].wait_send()

    for copy in copies_y_g + [
        copy_core_s, copy_core_f, copy_core_g, copy_z_s, copy_z_f,
        copy_zb_s, copy_zb_f, copy_zb_g, copy_cb_s, copy_cb_f,
    ]:
        copy.wait_send()


def body(space_n, *args):
    def kern(*refs):
        kernel(space_n, *refs)

    def vmem(*shape):
        return pltpu.VMEM(shape, F32)

    def sems(*shape):
        return pltpu.SemaphoreType.DMA(shape)

    start, grad_n, grad_k = pl.pallas_call(
        kern,
        out_shape=(
            jax.ShapeDtypeStruct((1, 11, 4, 2048), F32),
            jax.ShapeDtypeStruct((4, 128), F32),
            jax.ShapeDtypeStruct((8, 4, 128), F32),
        ),
        in_specs=[pl.BlockSpec(memory_space=pltpu.VMEM)] * 8,
        out_specs=[pl.BlockSpec(memory_space=pltpu.VMEM)] * 3,
        scratch_shapes=[
            vmem(4, 4, 2048), vmem(4, 4, 2048), vmem(4, 4, 2048), vmem(4, 4, 2048),
            vmem(4, 8, 4, 512), vmem(4, 8, 4, 512), vmem(4, 4, 4, 512),
            vmem(2, 4, 2, 9, 4, 128),
            vmem(4, 1, 2048), vmem(4, 2, 2048), vmem(4, 1, 2048), vmem(4, 2, 2048),
            vmem(2, 8, 4, 512), vmem(2, 4, 4, 512), vmem(2, 8, 4, 512), vmem(2, 4, 4, 512),
            vmem(8, 4, 512), vmem(4, 4, 512), vmem(8, 4, 512), vmem(4, 4, 512),
            vmem(3, 8, 4, 512), vmem(3, 4, 4, 512),
            vmem(8, 4, 512), vmem(3, 4, 512), vmem(8, 4, 512), vmem(3, 4, 512),
            vmem(2, 8, 4, 512), vmem(2, 3, 4, 512),
            vmem(2, 8, 4, 512), vmem(2, 3, 4, 512), vmem(2, 8, 4, 512), vmem(2, 3, 4, 512),
            vmem(4, 2, 9, 4, 128), vmem(4, 2, 9, 4, 128), vmem(3, 2, 9, 4, 128),
            vmem(2, 9, 4, 128), vmem(9, 4, 128),
            sems(4, 4), sems(2, 3), sems(2, 2), sems(2, 2, 3), sems(2, 3), sems(2, 3),
            sems(2, 2),
        ],
        compiler_params=pltpu.CompilerParams(collective_id=0, has_side_effects=True),
    )(*args)
    return start, grad_n, grad_k


def solution(mesh):
    space_n = mesh.shape["space"]

    def local(*args):
        return body(space_n, *args)

    return jax.shard_map(
        local,
        mesh=mesh,
        in_specs=(
            P("tm", None, "space", None),
            P("tm", None, "space", None),
            P("tm", None, None, "space", None),
            P("tm", None, None, "space", None),
            P("tm", "space", None),
            P("space", None),
            P("space", None),
            P(None, "space", None),
        ),
        out_specs=(P("tm", None, "space", None), P("space", "tm"), P(None, "space", "tm")),
        check_vma=False,
    )
```

time: 397 us -> 65 us (0.16)
  the two profiles are of different devices: /device:TPU:1 before, /device:TPU:103 now
where the time goes in v1:
time: 65 us; the launch traced here: 64.9 us
  Pallas kernels  61.3 us (94%)
  local copies, waits for them, and re-layouts  2.94 us (5%)
  between operations  0.66 us (1%)
    pallas_call x1, Pallas kernels, body(): pl.pallas_call(kern, out_shape=(jax.ShapeDtypeStruct((1, 11, 4, 2048), F3...  61.3 us
    unnamed x7, local copies, waits for them, and re-layouts  2.94 us

profile of v1, /device:TPU:103, one launch (start us, length us, event | category | flops | bytes accessed | tf_op | source)
XLA Modules:
  0.0 64.9 jit_solution(11926718417428002113)
XLA Ops:
  0.6 61.3 %shard_map.103 = (f32[1,11,4,2048]{3,2,1,0:T(4,128)}, f32[4,128]{1,0:T(4,128)}, f32[8,4,128]{2,1,0:T(4,128)}) custom-call(f32[1,11,4,2048]{3,2,1,0:T(4,128)} %refs_0_.1, f32[1,4,4,2048]{3,2,1,0:T(4,128)} %refs_1_.1, f32[1,4,2,4,2048]{4,3,2,1,0:T(4,128)} %refs_2_.1, bf16[1,4,8,4,2048]{4,3,2,1,0:T(4,128)(2,1)} %refs_3_.1, s32[1,4,2048]{2,1,0:T(4,128)} %refs_4_.1, ...), custom_call_target="tpu_custom_call" | custom-call | tf_op jit(solution)/shard_map/pallas_call | solution.py:411
  61.9 0.0 copy-start.1
  61.9 0.0 copy-start
  61.9 1.8 %copy.14 = f32[1,11,4,2048]{3,2,1,0:T(4,128)} copy(f32[1,11,4,2048]{3,2,1,0:T(4,128)} %get-tuple-element.6) | data formatting | bytes 720896
  63.7 0.0 copy-done.1
  63.7 0.6 copy.15
  64.3 0.0 copy-done
  64.3 0.6 copy.16
Async XLA Ops:
  61.9 1.8 %copy-start.1 = (f32[4,128]{1,0:T(4,128)S(1)}, f32[4,128]{1,0:T(4,128)}, u32[]{:S(2)}) copy-start(f32[4,128]{1,0:T(4,128)} %get-tuple-element.7) | copy-start | bytes 6148
  61.9 2.3 %copy-start = (f32[8,4,128]{2,1,0:T(4,128)S(1)}, f32[8,4,128]{2,1,0:T(4,128)}, u32[]{:S(2)}) copy-start(f32[8,4,128]{2,1,0:T(4,128)} %get-tuple-element.8) | copy-start | bytes 49156

commit v2 on v1

v2 whole, which is shorter than its diff:
```python
import jax
import jax.numpy as jnp
from jax import lax
from jax.experimental import pallas as pl
from jax.experimental.pallas import tpu as pltpu
from jax.sharding import PartitionSpec as P

TIME_STEP = 0.4
GRAVITY = 9.81
MESH = pl.DeviceIdType.MESH
F32 = jnp.float32


def remote(src, dst, send_sem, recv_sem, device):
    return pltpu.make_async_remote_copy(
        src_ref=src, dst_ref=dst, send_sem=send_sem, recv_sem=recv_sem,
        device_id=device, device_id_type=MESH,
    )


def kernel(
    space_n, end_hbm, depth_hbm, vel_hbm, salt_hbm, wet_hbm, cls_hbm, man_hbm, cond_hbm,
    out_ref, gn_ref, gk_ref,
    end_ref, depth_ref, vel_ref, salt_ref, wet_ref, cls_ref, man_ref, cond_ref,
    damp, hdamp, gcoef, source, fac_s, grads,
    down_out, up_out, down_in, up_in,
    off_0, core_0, pair_0, z_0, quad_0, y_0, back_0, home_0,
    off_1, core_1, pair_1, z_1, quad_1, y_1, back_1, home_1,
    off_f, core_f, pair_f, z_f, quad_f, y_f, back_f, home_f,
    core_g, sum_g, y_g, z_g_out, z_g,
    in_sems, halo_sems, core_sems, z_sems, y_sems, back_sems,
):
    sp = lax.axis_index("space")
    w = lax.axis_index("tm")
    core = lax.rem(w, 2)
    zh = lax.rem(lax.div(w, 2), 2)
    y = lax.div(w, 4)
    core_peer = (sp, w + 1 - 2 * core)
    z_peer = (sp, w + 2 - 4 * zh)
    has_prev = sp > 0
    has_next = sp < space_n - 1

    def y_peer(d):
        return (sp, lax.rem(w + 4 * d, 16))

    barrier = pltpu.get_barrier_semaphore()
    for peer in (z_peer, core_peer, y_peer(1), y_peer(2), y_peer(3)):
        pl.semaphore_signal(barrier, inc=1, device_id=peer, device_id_type=MESH)

    @pl.when(has_prev)
    def _():
        pl.semaphore_signal(barrier, inc=1, device_id=(sp - 1, w), device_id_type=MESH)

    @pl.when(has_next)
    def _():
        pl.semaphore_signal(barrier, inc=1, device_id=(sp + 1, w), device_id_type=MESH)

    loads = []
    for at, (src, dst) in enumerate((
        (end_hbm, end_ref), (depth_hbm, depth_ref), (vel_hbm, vel_ref), (salt_hbm, salt_ref),
        (wet_hbm, wet_ref), (cls_hbm, cls_ref), (man_hbm, man_ref), (cond_hbm, cond_ref),
    )):
        load = pltpu.make_async_copy(src, dst, in_sems.at[at])
        load.start()
        loads.append(load)

    last = jnp.where(w == 15, 1.0, 0.0).astype(F32)

    for d in (1, 2, 3):
        @pl.when(y + d > 3)
        def _(d=d):
            for slots in (y_0, y_1, y_f):
                slots[d - 1] = jnp.zeros(slots.shape[1:], F32)

    @pl.when(sp == 0)
    def _():
        down_in[...] = jnp.zeros(down_in.shape, F32)

    @pl.when(sp == space_n - 1)
    def _():
        up_in[...] = jnp.zeros(up_in.shape, F32)

    for load in loads:
        load.wait()

    def chunk(i, carry):
        block = lax.div(i, 4)
        g_core = lax.rem(i, 2)
        g_zh = lax.rem(lax.div(i, 2), 2)
        cols = pl.ds(pl.multiple_of(i * 128, 128), 128)
        sub = pl.ds(pl.multiple_of(lax.rem(i, 4) * 128, 128), 128)
        wet = wet_ref[0, :, cols].astype(F32)
        infil = TIME_STEP * wet * (0.25 + 0.75 * cls_ref[:, cols].astype(F32))
        man = man_ref[:, cols]
        cond = cond_ref[:, :, cols]
        mu = end_ref[0, 3:, :, cols]
        zero = jnp.zeros_like(mu[:1])
        cond_above = jnp.concatenate([zero, cond[:-1]], 0)
        factor = 1.0 / (1.0 + 4 * TIME_STEP * (cond + cond_above))
        gk = jnp.zeros_like(mu)
        start = mu
        for k in (3, 2, 1, 0):
            h = depth_ref[0, k, :, cols]
            u = vel_ref[0, k, 0, :, cols]
            v = vel_ref[0, k, 1, :, cols]
            speed = jnp.sqrt(u * u + v * v)
            powered = jnp.exp(4.0 / 3.0 * jnp.log(h))
            rate = GRAVITY * man * man * speed / powered
            relaxed = 1.0 + TIME_STEP * rate
            damping = wet / relaxed
            damp[k, :, cols] = damping
            hdamp[k, :, cols] = h * damping
            gcoef[k, :, cols] = (
                -2.0 * TIME_STEP * GRAVITY * man * speed * damping / (powered * relaxed)
            )
            if k == 0:
                off_0[block, 4, :, sub] = wet / (1.0 + 4 * TIME_STEP * rate)
            source[k, :, cols] = infil * mu[0]
            salt = salt_ref[0, k, :, :, cols].astype(F32)
            salt_below = jnp.concatenate([salt[1:], zero], 0)
            mu_below = jnp.concatenate([mu[1:], zero], 0)
            diff = mu_below - mu
            gk = gk - TIME_STEP * (salt_below - salt) * diff
            flux = cond * diff
            mu = mu + TIME_STEP * (flux - jnp.concatenate([zero, flux[:-1]], 0))
        held = factor * start
        offset = mu - held
        offset = offset + last * held
        off_0[block, 0:4, :, sub] = offset[0:4]
        off_1[block, :, :, sub] = offset[4:8]
        fac_s[block, :, :, sub] = factor
        grads[g_core, block, g_zh, 0:8] = gk
        return carry

    lax.fori_loop(0, 16, chunk, 0)

    pl.semaphore_wait(
        barrier, 5 + jnp.where(has_prev, 1, 0) + jnp.where(has_next, 1, 0)
    )

    other_half = pl.ds(2 * (1 - core), 2)
    waves = (
        (off_0, core_0, pair_0, z_0, quad_0, y_0, back_0, home_0),
        (off_1, core_1, pair_1, z_1, quad_1, y_1, back_1, home_1),
        (off_f, core_f, pair_f, z_f, quad_f, y_f, back_f, home_f),
    )
    core_copies = [
        remote(v[0].at[other_half], v[1], core_sems.at[0, i], core_sems.at[1, i], core_peer)
        for i, v in enumerate(waves)
    ]
    z_copies = [
        remote(v[2], v[3], z_sems.at[0, i], z_sems.at[1, i], z_peer)
        for i, v in enumerate(waves)
    ]
    y_copies = [
        [
            remote(v[4], v[5].at[d - 1], y_sems.at[0, i, d - 1], y_sems.at[1, i, d - 1],
                   y_peer(4 - d))
            for d in (1, 2, 3)
        ]
        for i, v in enumerate(waves)
    ]
    back_copies = [
        remote(v[6], v[7], back_sems.at[0, i], back_sems.at[1, i], core_peer)
        for i, v in enumerate(waves)
    ]

    def core_flow(b):
        mine = off_0[2 * core + b, 4]
        theirs = core_0[b, 4]
        return jnp.where(core == 0, mine, theirs), jnp.where(core == 0, theirs, mine)

    def z_flow(b):
        mine = pair_0[b, 4]
        theirs = z_0[b, 4]
        return jnp.where(zh == 0, mine, theirs), jnp.where(zh == 0, theirs, mine)

    def factors(i, b):
        return fac_s[2 * core + b, 4 * i : 4 * i + 4]

    def make_pair(i):
        off, arrived, pair = waves[i][:3]
        core_copies[i].wait_recv()
        for b in range(2):
            mine = off[2 * core + b]
            theirs = arrived[b]
            earlier = jnp.where(core == 0, mine, theirs)
            later = jnp.where(core == 0, theirs, mine)
            if i == 2:
                factor, _ = core_flow(b)
                pair[b, 0] = earlier[0] + later[0]
                pair[b, 1:3] = earlier[1:3] + factor[None] * later[1:3]
            else:
                pair[b, 0:4] = earlier[0:4] + factors(i, b) * later[0:4]
                if i == 0:
                    pair[b, 4] = earlier[4] * later[4]
        z_copies[i].start()

    def make_quad(i):
        pair, arrived, quad = waves[i][2:5]
        z_copies[i].wait_recv()
        for b in range(2):
            mine = pair[b]
            theirs = arrived[b]
            earlier = jnp.where(zh == 0, mine, theirs)
            later = jnp.where(zh == 0, theirs, mine)
            if i == 2:
                factor, _ = z_flow(b)
                quad[b, 0] = earlier[0] + later[0]
                quad[b, 1:3] = earlier[1:3] + factor[None] * later[1:3]
            else:
                factor = factors(i, b)
                quad[b, 0:4] = earlier[0:4] + factor * factor * later[0:4]
                if i == 0:
                    quad[b, 4] = earlier[4] * later[4]
        for d in (1, 2, 3):
            @pl.when(y >= d)
            def _(d=d):
                y_copies[i][d - 1].start()

    def results(i, block, offset, ends):
        cols = pl.ds(pl.multiple_of(block * 512, 512), 512)
        if i == 2:
            out_ref[0, 0, :, cols] = offset[0] + ends[0]
            out_ref[0, 1:3, :, cols] = offset[1:3] + off_0[block, 4][None] * ends[1:3]
        else:
            factor = fac_s[block, 4 * i : 4 * i + 4]
            out_ref[0, 3 + 4 * i : 7 + 4 * i, :, cols] = offset[0:4] + factor * ends

    def make_ends(i):
        off, arrived, pair, z_arrived, _, slots, back = waves[i][:7]
        for d in (1, 2, 3):
            @pl.when(y + d <= 3)
            def _(d=d):
                y_copies[i][d - 1].wait_recv()
        own_ends = []
        for b in range(2):
            mine = off[2 * core + b]
            first = jnp.where(core == 0, arrived[b], mine)
            second = jnp.where(zh == 0, z_arrived[b], pair[b])
            if i == 2:
                _, core_factor = core_flow(b)
                _, z_factor = z_flow(b)

                def through(factor, map_, end):
                    return jnp.concatenate(
                        [map_[0:1] + end[0:1], map_[1:3] + factor[None] * end[1:3]], 0
                    )

                at_second = through(y_0[1, b, 4], slots[1, b], slots[2, b])
                at_second = through(y_0[0, b, 4], slots[0, b], at_second)
                at_first = through(z_factor, second, at_second)
                late = jnp.where(zh == 0, at_first, at_second)
                early = through(core_factor, first, late)
            else:
                factor = factors(i, b)
                two = factor * factor
                four = two * two
                at_second = slots[0, b, 0:4] + four * (
                    slots[1, b, 0:4] + four * slots[2, b, 0:4]
                )
                at_first = second[0:4] + two * at_second
                late = jnp.where(zh == 0, at_first, at_second)
                early = first[0:4] + factor * late
            back[b] = jnp.where(core == 0, late, early)
            own_ends.append((mine, jnp.where(core == 0, early, late)))
        back_copies[i].start()
        for b, (mine, ends) in enumerate(own_ends):
            results(i, 2 * core + b, mine, ends)

    def finish(i):
        back_copies[i].wait_recv()
        for b in range(2):
            block = 2 * (1 - core) + b
            results(i, block, waves[i][0][block], waves[i][7][b])

    core_copies[0].start()
    core_copies[1].start()

    level = end_ref[0, 0]
    flow_x = end_ref[0, 1]
    flow_y = end_ref[0, 2]
    wet = wet_ref[0].astype(F32)
    n_cols = level.shape[1]
    grad_n = jnp.zeros_like(level)
    halo_copies = []

    def left(value):
        lanes = lax.broadcasted_iota(jnp.int32, value.shape, 1)
        return jnp.where(lanes == 0, 0.0, pltpu.roll(value, 1, 1))

    def right(value):
        lanes = lax.broadcasted_iota(jnp.int32, value.shape, 1)
        return jnp.where(lanes == n_cols - 1, 0.0, pltpu.roll(value, n_cols - 1, 1))

    def without_above(k, level, flow_x, flow_y):
        hdx = hdamp[k] * flow_x
        hdy = hdamp[k] * flow_y
        return hdx, level + TIME_STEP * hdx + TIME_STEP * (hdy - left(hdy))

    def advance(k, partial, hdx, above, below, flow_x, flow_y):
        mid = partial - TIME_STEP * jnp.concatenate([above, hdx[0:3]], 0)
        wet_mid = wet * mid
        after = jnp.concatenate([wet_mid[1:4], below], 0)
        damping = damp[k]
        return (
            mid + source[k],
            damping * flow_x + TIME_STEP * (after - wet_mid),
            damping * flow_y + TIME_STEP * (right(wet_mid) - wet_mid),
            wet_mid,
        )

    def friction_term(k, flow_x, flow_y):
        return gcoef[k] * (vel_ref[0, k, 0] * flow_x + vel_ref[0, k, 1] * flow_y)

    for turn, (k, k_next) in enumerate(((3, 2), (1, 0))):
        hdx, partial = without_above(k, level, flow_x, flow_y)
        first, second, third, fourth = (slice(r, r + 1) for r in range(4))
        wet_mid_3 = wet[fourth] * (partial[fourth] - TIME_STEP * hdx[third])
        held_x = damp[k] * flow_x
        hd_next = hdamp[k_next]
        down_out[turn, 0:1] = hdx[fourth]
        down_out[turn, 1:2] = hd_next[fourth] * (held_x[fourth] - TIME_STEP * wet_mid_3)
        down_out[turn, 2:3] = TIME_STEP * hd_next[fourth]
        wet_mid_0 = wet[first] * partial[first]
        wet_mid_1 = wet[second] * (partial[second] - TIME_STEP * hdx[first])
        row_x = held_x[first] + TIME_STEP * (wet_mid_1 - wet_mid_0)
        row_y = damp[k, 0:1] * flow_y[first] + TIME_STEP * (right(wet_mid_0) - wet_mid_0)
        row_hdy = hd_next[first] * row_y
        up_out[turn, 0:1] = wet_mid_0
        up_out[turn, 1:2] = wet[first]
        up_out[turn, 2:3] = (
            partial[first] + source[k, 0:1] + TIME_STEP * hd_next[first] * row_x
            + TIME_STEP * (row_hdy - left(row_hdy))
        )
        up_out[turn, 3:4] = hd_next[first]
        down = remote(
            down_out.at[turn], down_in.at[turn],
            halo_sems.at[0, turn], halo_sems.at[1, turn], (sp + 1, w),
        )
        up = remote(
            up_out.at[turn], up_in.at[turn],
            halo_sems.at[2, turn], halo_sems.at[3, turn], (sp - 1, w),
        )
        halo_copies.append((down, up))

        @pl.when(has_next)
        def _(down=down):
            down.start()

        @pl.when(has_prev)
        def _(up=up):
            up.start()

        if turn == 0:
            make_pair(0)
            make_pair(1)
        grad_n = grad_n + friction_term(k, flow_x, flow_y)

        @pl.when(has_prev)
        def _(down=down):
            down.wait_recv()

        @pl.when(has_next)
        def _(up=up):
            up.wait_recv()

        wet_4 = up_in[turn, 1:2]
        hd_4 = up_in[turn, 3:4]
        added = -TIME_STEP * hdx[fourth]
        wet_added = wet_4 * added
        added_y = hd_4 * (TIME_STEP * (right(wet_added) - wet_added))
        partial_4 = (
            up_in[turn, 2:3] + added - TIME_STEP * TIME_STEP * hd_4 * wet_added
            + TIME_STEP * (added_y - left(added_y))
        )
        level, flow_x, flow_y, wet_mid = advance(
            k, partial, hdx, down_in[turn, 0:1], up_in[turn, 0:1] + wet_added, flow_x, flow_y
        )
        grad_n = grad_n + friction_term(k_next, flow_x, flow_y)
        hdx, partial = without_above(k_next, level, flow_x, flow_y)
        above = down_in[turn, 1:2] + down_in[turn, 2:3] * wet_mid[first]
        below = wet_4 * (partial_4 - TIME_STEP * hdx[fourth])
        level, flow_x, flow_y, _ = advance(
            k_next, partial, hdx, above, below, flow_x, flow_y
        )

    for b in range(4):
        cols = slice(b * 512, b * 512 + 512)
        factor = off_0[b, 4]
        off_f[b, 0] = level[:, cols] - (1.0 - last) * end_ref[0, 0, :, cols]
        off_f[b, 1] = flow_x[:, cols] - (1.0 - last) * factor * end_ref[0, 1, :, cols]
        off_f[b, 2] = flow_y[:, cols] - (1.0 - last) * factor * end_ref[0, 2, :, cols]
    core_copies[2].start()
    for i in range(16):
        grads[i % 2, i // 4, i // 2 % 2, 8] = grad_n[:, i * 128 : i * 128 + 128]
    copy_core_g = remote(
        grads.at[1 - core], core_g, core_sems.at[0, 3], core_sems.at[1, 3], core_peer
    )
    copy_core_g.start()

    make_pair(2)
    copy_core_g.wait_recv()
    sum_g[...] = grads[core] + core_g[...]
    copies_y_g = []
    for d in (1, 2, 3):
        copy = remote(
            sum_g.at[lax.rem(y + d, 4)], y_g.at[d - 1],
            y_sems.at[0, 3, d - 1], y_sems.at[1, 3, d - 1], y_peer(d),
        )
        copy.start()
        copies_y_g.append(copy)
    copy_z_g = remote(z_g_out.at[1 - zh], z_g, z_sems.at[0, 3], z_sems.at[1, 3], z_peer)

    make_quad(0)
    make_quad(1)
    total = sum_g[y]
    for d in (1, 2, 3):
        copies_y_g[d - 1].wait_recv()
        total = total + y_g[d - 1]
    z_g_out[...] = total
    copy_z_g.start()
    make_ends(0)
    make_quad(2)
    make_ends(1)
    copy_z_g.wait_recv()
    total = z_g_out[zh] + z_g[...]
    gk_ref[...] = total[0:8]
    gn_ref[...] = total[8]
    finish(0)
    make_ends(2)
    finish(1)
    finish(2)

    for down, up in halo_copies:
        @pl.when(has_next)
        def _(down=down):
            down.wait_send()

        @pl.when(has_prev)
        def _(up=up):
            up.wait_send()

    for d in (1, 2, 3):
        @pl.when(y >= d)
        def _(d=d):
            for copies in y_copies:
                copies[d - 1].wait_send()

    for copy in core_copies + z_copies + back_copies + copies_y_g + [copy_core_g, copy_z_g]:
        copy.wait_send()


def body(space_n, *args):
    def kern(*refs):
        kernel(space_n, *refs)

    def vmem(*shape):
        return pltpu.VMEM(shape, F32)

    def sems(*shape):
        return pltpu.SemaphoreType.DMA(shape)

    def wave(maps, ends):
        return [
            vmem(4, maps, 4, 512), vmem(2, maps, 4, 512), vmem(2, maps, 4, 512),
            vmem(2, maps, 4, 512), vmem(2, maps, 4, 512), vmem(3, 2, maps, 4, 512),
            vmem(2, ends, 4, 512), vmem(2, ends, 4, 512),
        ]

    start, grad_n, grad_k = pl.pallas_call(
        kern,
        out_shape=(
            jax.ShapeDtypeStruct((1, 11, 4, 2048), F32),
            jax.ShapeDtypeStruct((4, 128), F32),
            jax.ShapeDtypeStruct((8, 4, 128), F32),
        ),
        in_specs=[pl.BlockSpec(memory_space=pl.ANY)] * 8,
        out_specs=[pl.BlockSpec(memory_space=pltpu.VMEM)] * 3,
        scratch_shapes=[
            *[pltpu.VMEM(a.shape, a.dtype) for a in args],
            vmem(4, 4, 2048), vmem(4, 4, 2048), vmem(4, 4, 2048), vmem(4, 4, 2048),
            vmem(4, 8, 4, 512), vmem(2, 4, 2, 9, 4, 128),
            vmem(2, 3, 2048), vmem(2, 4, 2048), vmem(2, 3, 2048), vmem(2, 4, 2048),
            *wave(5, 4), *wave(4, 4), *wave(3, 3),
            vmem(4, 2, 9, 4, 128), vmem(4, 2, 9, 4, 128), vmem(3, 2, 9, 4, 128),
            vmem(2, 9, 4, 128), vmem(9, 4, 128),
            sems(8), sems(4, 2), sems(2, 4), sems(2, 4), sems(2, 4, 3), sems(2, 3),
        ],
        compiler_params=pltpu.CompilerParams(collective_id=0, has_side_effects=True),
    )(*args)
    return start, grad_n, grad_k


def solution(mesh):
    space_n = mesh.shape["space"]

    def local(*args):
        return body(space_n, *args)

    return jax.shard_map(
        local,
        mesh=mesh,
        in_specs=(
            P("tm", None, "space", None),
            P("tm", None, "space", None),
            P("tm", None, None, "space", None),
            P("tm", None, None, "space", None),
            P("tm", "space", None),
            P("space", None),
            P("space", None),
            P(None, "space", None),
        ),
        out_specs=(P("tm", None, "space", None), P("space", "tm"), P(None, "space", "tm")),
        check_vma=False,
    )
```

time: 65 us -> 54.2 us (0.83)
  the two profiles are of different devices: /device:TPU:103 before, /device:TPU:39 now
where the time goes in v2:
time: 54.2 us; the launch traced here: 54 us
  Pallas kernels  50.4 us (93%)
  local copies, waits for them, and re-layouts  2.94 us (5%)
  between operations  0.66 us (1%)
    pallas_call x1, Pallas kernels, body(): pl.pallas_call(kern, out_shape=(jax.ShapeDtypeStruct((1, 11, 4, 2048), F3...  50.4 us
    unnamed x7, local copies, waits for them, and re-layouts  2.94 us

profile of v2, /device:TPU:39, one launch (start us, length us, event | category | flops | bytes accessed | tf_op | source)
XLA Modules:
  0.0 54.0 jit_solution(18269115882158324086)
XLA Ops:
  0.6 50.4 %shard_map.103 = (f32[1,11,4,2048]{3,2,1,0:T(4,128)}, f32[4,128]{1,0:T(4,128)}, f32[8,4,128]{2,1,0:T(4,128)}) custom-call(f32[1,11,4,2048]{3,2,1,0:T(4,128)} %refs_0_.1, f32[1,4,4,2048]{3,2,1,0:T(4,128)} %refs_1_.1, f32[1,4,2,4,2048]{4,3,2,1,0:T(4,128)} %refs_2_.1, bf16[1,4,8,4,2048]{4,3,2,1,0:T(4,128)(2,1)} %refs_3_.1, s32[1,4,2048]{2,1,0:T(4,128)} %refs_4_.1, ...), custom_call_target="tpu_custom_call" | custom-call | tf_op jit(solution)/shard_map/pallas_call | solution.py:471
  51.0 0.0 copy-start.1
  51.0 0.0 copy-start
  51.0 1.8 %copy.14 = f32[1,11,4,2048]{3,2,1,0:T(4,128)} copy(f32[1,11,4,2048]{3,2,1,0:T(4,128)} %get-tuple-element.6) | data formatting | bytes 720896
  52.8 0.0 copy-done.1
  52.8 0.6 %copy.15 = f32[4,128]{1,0:T(4,128)} copy(f32[4,128]{1,0:T(4,128)S(1)} %copy-done.1) | data formatting | bytes 4096
  53.4 0.0 copy-done
  53.4 0.6 %copy.16 = f32[8,4,128]{2,1,0:T(4,128)} copy(f32[8,4,128]{2,1,0:T(4,128)S(1)} %copy-done) | data formatting | bytes 32768
Async XLA Ops:
  51.0 1.8 %copy-start.1 = (f32[4,128]{1,0:T(4,128)S(1)}, f32[4,128]{1,0:T(4,128)}, u32[]{:S(2)}) copy-start(f32[4,128]{1,0:T(4,128)} %get-tuple-element.7) | copy-start | bytes 6148
  51.0 2.3 %copy-start = (f32[8,4,128]{2,1,0:T(4,128)S(1)}, f32[8,4,128]{2,1,0:T(4,128)}, u32[]{:S(2)}) copy-start(f32[8,4,128]{2,1,0:T(4,128)} %get-tuple-element.8) | copy-start | bytes 49156

commit v3 on v2

--- a/solution.py
+++ b/solution.py
@@ -149,12 +149,12 @@
         for i, v in enumerate(waves)
     ]
     z_copies = [
-        remote(v[2], v[3], z_sems.at[0, i], z_sems.at[1, i], z_peer)
+        remote(v[4 if i == 1 else 2], v[3], z_sems.at[0, i], z_sems.at[1, i], z_peer)
         for i, v in enumerate(waves)
     ]
     y_copies = [
         [
-            remote(v[4], v[5].at[d - 1], y_sems.at[0, i, d - 1], y_sems.at[1, i, d - 1],
+            remote(v[2 if i == 1 else 4], v[5].at[d - 1], y_sems.at[0, i, d - 1], y_sems.at[1, i, d - 1],
                    y_peer(4 - d))
             for d in (1, 2, 3)
         ]
@@ -177,6 +177,31 @@
 
     def factors(i, b):
         return fac_s[2 * core + b, 4 * i : 4 * i + 4]
+
+    def start_y(i):
+        for d in (1, 2, 3):
+            @pl.when(y >= d)
+            def _(d=d):
+                y_copies[i][d - 1].start()
+
+    def wait_y(i):
+        for d in (1, 2, 3):
+            @pl.when(y + d <= 3)
+            def _(d=d):
+                y_copies[i][d - 1].wait_recv()
+
+    def later_pairs(b):
+        factor = factors(1, b)
+        two = factor * factor
+        four = two * two
+        return y_1[0, b] + four * (y_1[1, b] + four * y_1[2, b]), two, four
+
+    def z_of_wave_1():
+        wait_y(1)
+        for b in range(2):
+            later, _, four = later_pairs(b)
+            quad_1[b] = jnp.where(zh == 0, later, pair_1[b] + four * later)
+        z_copies[1].start()
 
     def make_pair(i):
         off, arrived, pair = waves[i][:3]
@@ -194,7 +219,10 @@
                 pair[b, 0:4] = earlier[0:4] + factors(i, b) * later[0:4]
                 if i == 0:
                     pair[b, 4] = earlier[4] * later[4]
-        z_copies[i].start()
+        if i == 1:
+            start_y(i)
+        else:
+            z_copies[i].start()
 
     def make_quad(i):
         pair, arrived, quad = waves[i][2:5]
@@ -213,10 +241,7 @@
                 quad[b, 0:4] = earlier[0:4] + factor * factor * later[0:4]
                 if i == 0:
                     quad[b, 4] = earlier[4] * later[4]
-        for d in (1, 2, 3):
-            @pl.when(y >= d)
-            def _(d=d):
-                y_copies[i][d - 1].start()
+        start_y(i)
 
     def results(i, block, offset, ends):
         cols = pl.ds(pl.multiple_of(block * 512, 512), 512)
@@ -229,10 +254,10 @@
 
     def make_ends(i):
         off, arrived, pair, z_arrived, _, slots, back = waves[i][:7]
-        for d in (1, 2, 3):
-            @pl.when(y + d <= 3)
-            def _(d=d):
-                y_copies[i][d - 1].wait_recv()
+        if i == 1:
+            z_copies[1].wait_recv()
+        else:
+            wait_y(i)
         own_ends = []
         for b in range(2):
             mine = off[2 * core + b]
@@ -252,6 +277,10 @@
                 at_first = through(z_factor, second, at_second)
                 late = jnp.where(zh == 0, at_first, at_second)
                 early = through(core_factor, first, late)
+            elif i == 1:
+                later, two, _ = later_pairs(b)
+                late = z_1[b] + two * later
+                early = first + factors(1, b) * late
             else:
                 factor = factors(i, b)
                 two = factor * factor
@@ -400,6 +429,7 @@
     copy_core_g.start()
 
     make_pair(2)
+    z_of_wave_1()
     copy_core_g.wait_recv()
     sum_g[...] = grads[core] + core_g[...]
     copies_y_g = []
@@ -413,7 +443,6 @@
     copy_z_g = remote(z_g_out.at[1 - zh], z_g, z_sems.at[0, 3], z_sems.at[1, 3], z_peer)
 
     make_quad(0)
-    make_quad(1)
     total = sum_g[y]
     for d in (1, 2, 3):
         copies_y_g[d - 1].wait_recv()
@@ -422,13 +451,13 @@
     copy_z_g.start()
     make_ends(0)
     make_quad(2)
+    finish(0)
     make_ends(1)
+    make_ends(2)
     copy_z_g.wait_recv()
     total = z_g_out[zh] + z_g[...]
     gk_ref[...] = total[0:8]
     gn_ref[...] = total[8]
-    finish(0)
-    make_ends(2)
     finish(1)
     finish(2)
 
@@ -449,6 +478,18 @@
 
     for copy in core_copies + z_copies + back_copies + copies_y_g + [copy_core_g, copy_z_g]:
         copy.wait_send()
+
+
+def hand_over(start_ref, grad_n_ref, grad_k_ref, start_out, grad_n_out, grad_k_out, sems):
+    copies = []
+    for at, (src, dst) in enumerate((
+        (start_ref, start_out), (grad_n_ref, grad_n_out), (grad_k_ref, grad_k_out)
+    )):
+        copy = pltpu.make_async_copy(src, dst, sems.at[at])
+        copy.start()
+        copies.append(copy)
+    for copy in copies:
+        copy.wait()
 
 
 def body(space_n, *args):
@@ -489,7 +530,13 @@
         ],
         compiler_params=pltpu.CompilerParams(collective_id=0, has_side_effects=True),
     )(*args)
-    return start, grad_n, grad_k
+    return pl.pallas_call(
+        hand_over,
+        out_shape=tuple(jax.ShapeDtypeStruct(a.shape, a.dtype) for a in (start, grad_n, grad_k)),
+        in_specs=[pl.BlockSpec(memory_space=pl.ANY)] * 3,
+        out_specs=[pl.BlockSpec(memory_space=pltpu.VMEM)] * 3,
+        scratch_shapes=[sems(3)],
+    )(start, grad_n, grad_k)
 
 
 def solution(mesh):

time: 54.2 us -> 49.5 us (0.913)
  local copies, waits for them, and re-layouts: 2.94 us -> 0 us
  Pallas kernels: 50.4 us -> 48.7 us
    pallas_call x1, Pallas kernels: 50.4 us -> 47 us  [body(): pl.pallas_call(kern, out_shape=(jax.ShapeDtypeStruct((1, 11, 4, 2048), F3...]
    unnamed x7 -> x0, local copies, waits for them, and re-layouts: 2.94 us -> none
    pallas_call x0 -> x1, Pallas kernels: none -> 1.76 us  [body(): pl.pallas_call(hand_over, out_shape=tuple((jax.ShapeDtypeStruct(a.shape,...]
where the time goes in v3:
time: 49.5 us; the launch traced here: 49.4 us
  Pallas kernels  48.7 us (98%)
  between operations  0.64 us (1%)
    pallas_call x1, Pallas kernels, body(): pl.pallas_call(kern, out_shape=(jax.ShapeDtypeStruct((1, 11, 4, 2048), F3...  47 us
    pallas_call x1, Pallas kernels, body(): pl.pallas_call(hand_over, out_shape=tuple((jax.ShapeDtypeStruct(a.shape,...  1.76 us

profile of v3, /device:TPU:39, one launch (start us, length us, event | category | flops | bytes accessed | tf_op | source)
XLA Modules:
  0.0 49.4 jit_solution(15145232200388718657)
XLA Ops:
  0.6 47.0 %shard_map.103 = (f32[1,11,4,2048]{3,2,1,0:T(4,128)}, f32[4,128]{1,0:T(4,128)}, f32[8,4,128]{2,1,0:T(4,128)}) custom-call(f32[1,11,4,2048]{3,2,1,0:T(4,128)} %refs_0_.1, f32[1,4,4,2048]{3,2,1,0:T(4,128)} %refs_1_.1, f32[1,4,2,4,2048]{4,3,2,1,0:T(4,128)} %refs_2_.1, bf16[1,4,8,4,2048]{4,3,2,1,0:T(4,128)(2,1)} %refs_3_.1, s32[1,4,2048]{2,1,0:T(4,128)} %refs_4_.1, ...), custom_call_target="tpu_custom_call" | custom-call | tf_op jit(solution)/shard_map/pallas_call | solution.py:512
  47.6 1.8 %shard_map.104 = (f32[1,11,4,2048]{3,2,1,0:T(4,128)}, f32[4,128]{1,0:T(4,128)}, f32[8,4,128]{2,1,0:T(4,128)}) custom-call(f32[1,11,4,2048]{3,2,1,0:T(4,128)} %get-tuple-element.6.start_ref, f32[4,128]{1,0:T(4,128)} %get-tuple-element.7.grad_n_ref, f32[8,4,128]{2,1,0:T(4,128)} %get-tuple-element.8.grad_k_ref), custom_call_target="tpu_custom_call" | custom-call | tf_op jit(solution)/shard_map/pallas_call | solution.py:533
